TPU v7x, 32 devices: a whole 2x2x4 slice. The times are simulated.
32 devices in a mesh: row: 4 (over y, x), col: 8 (over z, core).
Axes of the slice: x: 2, y: 2, z: 4, core: 2. Of those that a mesh axis runs over, the one named last changes fastest.
Arguments:
- integrals: bfloat16 [2880, 23040], P('row', 'col'), may hold values from -0.0390625 to 0.0390625
- amplitudes: bfloat16 [23040, 256], P('col', 'row'), may hold values from -6 to 6
Outputs:
- ladder: bfloat16 [256, 2880], P('col', 'row')
All inputs are finite; a program needn't handle non-finite values.
Results may differ from a plain program's by a relative error of at most 0.001.
Values may be sent and summed in bfloat16 or wider, within the bound.
A program may use at most 64 MiB of HBM per device.

v0:
```python
import functools

import jax
import jax.numpy as jnp
from jax import lax
from jax.experimental import pallas as pl
from jax.experimental.pallas import tpu as pltpu
from jax.sharding import PartitionSpec as P

MESH = pl.DeviceIdType.MESH
NT = (((1,), (1,)), ((), ()))


def cuts_of(size, pieces, step):
    width = -(-size // (pieces * step)) * step
    return [(at, min(width, size - at)) for at in range(0, size, width)]


def ladder_kernel(chips, cuts, v_ref, t_ref, out_ref, v, t, parts, swap, summed, landed,
                  v_sem, t_sem, near_send, near_recv, far_send, far_recv, late_send, late_recv, last_send, last_recv,
                  swap_send, swap_recv, line_send, line_recv):
    depth = t_ref.shape[1]
    half = t_ref.shape[0] // 2
    part = half // 2
    r, c = lax.axis_index("row"), lax.axis_index("col")
    z, core = c // 2, c % 2
    rx = r + 1 - 2 * (r % 2)
    ry = r + 2 - 4 * (r // 2)
    rd = 3 - r
    other = 1 - core
    own = (0, half, (r, r), 0)
    near = (2 * half, half, (rx, ry), 0)
    far = [(4 * half + 2 * part * j, part, (rd, rd), part * j) for j in range(2)]
    late = (6 * half, half, (ry, rx), 0)
    slots = [own, near, *far, late]

    t_copy = pltpu.make_async_copy(t_ref, t.at[pl.ds(0, 2 * half)], t_sem)
    t_copy.start()
    v_copies = []
    for i, (at, width) in enumerate(cuts):
        copy = pltpu.make_async_copy(v_ref.at[:, pl.ds(at, width)], v.at[:, pl.ds(at, width)], v_sem.at[i])
        copy.start()
        v_copies.append(copy)

    barrier = pltpu.get_barrier_semaphore()
    pl.semaphore_signal(barrier, inc=1, device_id={"row": rx}, device_id_type=MESH)
    pl.semaphore_signal(barrier, inc=1, device_id={"row": ry}, device_id_type=MESH)
    pl.semaphore_signal(barrier, inc=1, device_id={"col": 2 * z + other}, device_id_type=MESH)
    for step in range(1, chips):
        peer = lax.rem(z + step, chips)
        pl.semaphore_signal(barrier, inc=1, device_id={"col": 2 * peer + core}, device_id_type=MESH)
    pl.semaphore_wait(barrier, chips + 2)

    def send(source, target, to, sems):
        copy = pltpu.make_async_remote_copy(
            src_ref=source, dst_ref=target, send_sem=sems[0], recv_sem=sems[1],
            device_id={"row": to}, device_id_type=MESH)
        copy.start()
        return copy

    def at_rows(first, count):
        return t.at[pl.ds(first, count)]

    near_copies = []
    for j in range(2):
        for h, to in ((0, rx), (1, ry)):
            near_copies.append(send(
                t_ref.at[pl.ds(h * half + j * part, part)], at_rows(near[0] + h * half + j * part, part), to,
                (near_send.at[j, h], near_recv.at[j, h])))

    def relay(j):
        copies = []
        for h, to in ((0, ry), (1, rx)):
            copies.append(send(
                at_rows(near[0] + h * half + j * part, part), at_rows(far[j][0] + h * part, part), to,
                (far_send.at[j, h], far_recv.at[j, h])))
        return copies

    def multiply(slot, at, width):
        first, count = slot[0], 2 * slot[1]
        return lax.dot_general(
            t[first:first + count, at:at + width], v[:, at:at + width], NT, preferred_element_type=jnp.float32)

    def swap_start(i):
        first, count, _, _ = slots[i]
        copy = pltpu.make_async_remote_copy(
            src_ref=parts.at[pl.ds(first + other * count, count)], dst_ref=swap.at[pl.ds(first // 2, count)],
            send_sem=swap_send.at[i], recv_sem=swap_recv.at[i],
            device_id={"col": 2 * z + other}, device_id_type=MESH)
        copy.start()
        return copy

    def goal(i):
        one, two = slots[i][2]
        return one * other + two * core

    def line_copy(i):
        first, count, _, place = slots[i]
        return pltpu.make_async_remote_copy(
            src_ref=summed.at[pl.ds(first // 2, count)], dst_ref=landed.at[z, pl.ds(place, count)],
            send_sem=line_send.at[i], recv_sem=line_recv.at[z],
            device_id={"col": 2 * goal(i) + core}, device_id_type=MESH)

    def swap_finish(i, copy):
        first, count, _, place = slots[i]
        copy.wait_recv()
        total = parts[pl.ds(first + core * count, count)] + swap[first // 2:first // 2 + count]

        @pl.when(goal(i) == z)
        def _():
            landed[z, place:place + count] = total

        @pl.when(goal(i) != z)
        def _():
            summed[first // 2:first // 2 + count] = total
            line_copy(i).start()

    def store(i, value):
        first, count = slots[i][0], 2 * slots[i][1]
        parts[first:first + count] = value

    def wait(copies):
        for copy in copies:
            copy.wait_recv()

    t_copy.wait()
    total = None
    for i, (at, width) in enumerate(cuts):
        v_copies[i].wait()
        term = multiply(own, at, width)
        total = term if total is None else total + term
    store(0, total)
    swaps = [swap_start(0)]

    wait(near_copies[:2])
    far_copies = relay(0)
    swap_finish(0, swaps[0])
    wait(near_copies[2:])
    far_copies += relay(1)
    late_copies = []
    for h, to in ((1, rx), (0, ry)):
        late_copies.append(send(
            t_ref.at[pl.ds(h * half, part)], at_rows(late[0] + h * half, part), to,
            (late_send.at[h], late_recv.at[h])))
    last_copies = []
    for i, (at, width) in enumerate(cuts):
        for h, to in ((1, rx), (0, ry)):
            last_copies.append(send(
                t_ref.at[pl.ds(h * half + part, part), pl.ds(at, width)],
                t.at[pl.ds(late[0] + h * half + part, part), pl.ds(at, width)], to,
                (last_send.at[i, h], last_recv.at[i, h])))
    store(1, multiply(near, 0, depth))
    swaps.append(swap_start(1))

    wait(far_copies[:2])
    store(2, multiply(far[0], 0, depth))
    swaps.append(swap_start(2))
    swap_finish(1, swaps[1])

    wait(far_copies[2:])
    store(3, multiply(far[1], 0, depth))
    swaps.append(swap_start(3))
    swap_finish(2, swaps[2])

    wait(late_copies)
    total = None
    for i, (at, width) in enumerate(cuts):
        wait(last_copies[2 * i:2 * i + 2])
        term = multiply(late, at, width)
        total = term if total is None else total + term
        if i == 0:
            swap_finish(3, swaps[3])
    store(4, total)
    swaps.append(swap_start(4))
    swap_finish(4, swaps[4])

    for source in range(chips):
        @pl.when(z != source)
        def _():
            pltpu.make_async_copy(landed.at[source], landed.at[source], line_recv.at[source]).wait()
    total = landed[0]
    for source in range(1, chips):
        total = total + landed[source]
    out_ref[...] = total.astype(out_ref.dtype)

    for copy in near_copies + far_copies + late_copies + last_copies + swaps:
        copy.wait_send()
    for i in range(len(slots)):
        @pl.when(goal(i) != z)
        def _():
            line_copy(i).wait_send()


def ladder_on_chips(integrals, amplitudes):
    chips = lax.axis_size("col") // 2
    blocks = amplitudes.T
    pairs, depth = blocks.shape
    rows = integrals.shape[0]
    half = pairs // 2
    cuts = cuts_of(depth, 2, 256)
    f32 = jnp.float32
    dma = pltpu.SemaphoreType.DMA
    return pl.pallas_call(
        functools.partial(ladder_kernel, chips, cuts),
        out_shape=jax.ShapeDtypeStruct((half, rows), jnp.bfloat16),
        in_specs=[pl.BlockSpec(memory_space=pl.ANY)] * 2,
        out_specs=pl.BlockSpec(memory_space=pltpu.VMEM),
        scratch_shapes=[
            pltpu.VMEM((rows, depth), jnp.bfloat16),
            pltpu.VMEM((4 * pairs, depth), jnp.bfloat16),
            pltpu.VMEM((4 * pairs, rows), f32),
            pltpu.VMEM((2 * pairs, rows), f32),
            pltpu.VMEM((2 * pairs, rows), f32),
            pltpu.VMEM((chips, half, rows), f32),
            dma((len(cuts),)), dma,
            dma((2, 2)), dma((2, 2)),
            dma((2, 2)), dma((2, 2)),
            dma((2,)), dma((2,)),
            dma((len(cuts), 2)), dma((len(cuts), 2)),
            dma((5,)), dma((5,)),
            dma((5,)), dma((chips,)),
        ],
        compiler_params=pltpu.CompilerParams(
            collective_id=0, has_side_effects=True, vmem_limit_bytes=67043328),
    )(integrals, blocks)


def per_device(integrals, amplitudes):
    columns = lax.axis_size("col")
    if lax.axis_size("row") == 4 and columns == 8:
        return ladder_on_chips(integrals, amplitudes)
    gathered = lax.all_gather(amplitudes, "row", axis=1, tiled=True)
    product = lax.dot_general(
        gathered, integrals, (((0,), (1,)), ((), ())), preferred_element_type=jnp.float32)
    return lax.psum_scatter(product, "col", scatter_dimension=0, tiled=True).astype(jnp.bfloat16)


def solution(mesh):
    in_specs = (P("row", "col"), P("col", "row"))
    out_specs = P("col", "row")
    return jax.shard_map(
        per_device, mesh=mesh, in_specs=in_specs, out_specs=out_specs, check_vma=False
    )
```

profile of v0, /device:TPU:4, one launch (start us, length us, event | category | flops | bytes accessed | tf_op | source)
XLA Modules:
  0.0 28.1 jit_solution(1346194651075714808)
XLA Ops:
  0.0 26.7 %shard_map.28 = bf16[32,720]{1,0:T(8,128)(2,1)} custom-call(bf16[720,2880]{1,0:T(8,128)(2,1)} %v_ref.1, bf16[64,2880]{1,0:T(8,128)(2,1)} %bitcast.1), custom_call_target="tpu_custom_call" | custom-call | tf_op jit(solution)/shard_map/pallas_call | solution.py:203
  26.7 1.4 %copy.4 = bf16[32,720]{1,0:T(8,128)(2,1)} copy(bf16[32,720]{1,0:T(8,128)(2,1)} %shard_map.28) | data formatting | bytes 92160
where the time goes:
time: 28.3 us; the launch traced here: 28.1 us
  Pallas kernels  26.7 us (94%)
  local copies, waits for them, and re-layouts  1.42 us (5%)
    pallas_call x1, Pallas kernels, ladder_on_chips(): pl.pallas_call(functools.partial(ladder_kernel, chips, cuts), out_shape=j...  26.7 us
    unnamed x1, local copies, waits for them, and re-layouts  1.42 us

commit v1 on v0

v1 whole, which is shorter than its diff:
```python
import functools

import jax
import jax.numpy as jnp
from jax import lax
from jax.experimental import pallas as pl
from jax.experimental.pallas import tpu as pltpu
from jax.sharding import PartitionSpec as P

MESH = pl.DeviceIdType.MESH
NT = (((1,), (1,)), ((), ()))
SLOTS = 6
A1, A2, L1, L2, R1, R2 = range(6)


def cuts_of(size, pieces, step):
    width = -(-size // (pieces * step)) * step
    return [(at, min(width, size - at)) for at in range(0, size, width)]


def ladder_kernel(chips, cuts, v_ref, t_ref, out_ref, v, t, o_parts, o_swap, o_sum, parts, swap, summed, landed,
                  v_sem, t_sem, sent, came, swap_send, swap_recv, line_send, line_recv, known):
    pairs = t_ref.shape[0]
    q = pairs // 4
    r, c = lax.axis_index("row"), lax.axis_index("col")
    z, core = c // 2, c % 2
    rx = r + 1 - 2 * (r % 2)
    ry = r + 2 - 4 * (r // 2)
    rd = 3 - r
    partner = 2 * z + 1 - core
    above, below = z < chips - 1, z > 0
    x_own_last = (r // 2) == (z // 2)
    y_own_last = (r % 2) == (z % 2)

    t_copy = pltpu.make_async_copy(t_ref, t.at[pl.ds(0, pairs)], t_sem)
    t_copy.start()
    v_copies = []
    for i, (at, width) in enumerate(cuts):
        copy = pltpu.make_async_copy(v_ref.at[:, pl.ds(at, width)], v.at[:, pl.ds(at, width)], v_sem.at[i])
        copy.start()
        v_copies.append(copy)

    barrier = pltpu.get_barrier_semaphore()

    def signal(sem, **to):
        pl.semaphore_signal(sem, inc=1, device_id=to, device_id_type=MESH)

    def signal_line(up, down):
        @pl.when(above)
        def _():
            signal(up, col=c + 2)

        @pl.when(below)
        def _():
            signal(down, col=c - 2)

    signal(barrier, row=rx)
    signal(barrier, row=ry)
    signal(barrier, col=partner)
    signal_line(barrier, barrier)
    pl.semaphore_wait(barrier, 5 - jnp.where(above, 0, 1) - jnp.where(below, 0, 1))

    lies = ([pairs, pairs + q, pairs + 2 * q, pairs + 3 * q, 3 * pairs + 2 * q, 3 * pairs + 3 * q],
            [2 * pairs + 2 * q, 2 * pairs + 3 * q, 2 * pairs, 2 * pairs + q, 3 * pairs, 3 * pairs + q])
    own_rows = ([0, q, 2 * q, 3 * q], [2 * q, 3 * q, 0, q])
    to_row = (rx, ry)

    def item_copies(link, item):
        copies = []
        whole = [(0, t_ref.shape[1])] if item < L2 else cuts
        for n, (at, width) in enumerate(whole):
            columns = pl.ds(at, width)
            if item <= L2:
                source = t_ref.at[pl.ds(own_rows[link][item], q), columns]
            else:
                source = t.at[pl.ds(lies[1 - link][item - R1], q), columns]
            copies.append(pltpu.make_async_remote_copy(
                src_ref=source, dst_ref=t.at[pl.ds(lies[link][item], q), columns],
                send_sem=sent.at[link, item, n], recv_sem=came.at[link, item, n],
                device_id={"row": to_row[link]}, device_id_type=MESH))
        return copies

    items = [[item_copies(link, item) for item in range(6)] for link in range(2)]

    def start(link, item):
        for copy in items[link][item]:
            copy.start()

    for item in (A1, A2, L1):
        for link in range(2):
            start(link, item)
    own_last = (x_own_last, y_own_last)
    for link in range(2):
        @pl.when(jnp.logical_not(own_last[link]))
        def _():
            start(link, L2)
    signal_line(known.at[0], known.at[1])

    def heard(first, second):
        @pl.when(below)
        def _():
            pl.semaphore_wait(known.at[first], 1)

        @pl.when(above)
        def _():
            pl.semaphore_wait(known.at[second], 1)

    def slot_items(s):
        if s < 3:
            return [s, s]
        last, early = ((R1, L2), (R2, R1), (L2, R2))[s - 3]
        return [jnp.where(own_last[link], last, early) for link in range(2)]

    def pick(table, item):
        if isinstance(item, int):
            return table[item]
        at = table[-1]
        for n in range(len(table) - 2, L2 - 1, -1):
            at = jnp.where(item == n, table[n], at)
        return pl.multiple_of(at, q)

    def arrive(s, n):
        for link, item in enumerate(slot_items(s)):
            rows = t.at[pl.ds(pick(lies[link], item), q)]
            if n is None:
                held = rows
                pltpu.make_async_copy(held, held, came.at[link, item, 0]).wait()
            else:
                at, width = cuts[n]
                held = rows.at[:, pl.ds(at, width)]
                pltpu.make_async_copy(held, held, came.at[link, item, n]).wait()

    def low_link(s):
        return 0 if s < 2 else 1

    def multiply(s, at, width):
        found = slot_items(s)
        low = low_link(s)
        rows = [t[pl.ds(pick(lies[link], found[link]), q), at:at + width] for link in (low, 1 - low)]
        return lax.dot_general(
            jnp.concatenate(rows, axis=0), v[:, at:at + width], NT, preferred_element_type=jnp.float32)

    def kept(s):
        found = slot_items(s)
        low = low_link(s)
        beside = (rx, ry)

        def goal(link):
            if isinstance(found[link], int):
                return beside[link]
            return jnp.where(found[link] >= R1, rd, beside[link])

        def place(link):
            return (found[link] % 2) * q

        where = jnp.where(core == 0, goal(low), goal(1 - low))
        spot = jnp.where(core == 0, place(low), place(1 - low))
        return where, pl.multiple_of(spot, q)

    def swap_copy(s):
        if s is None:
            source, target, n = o_parts.at[1 - core], o_swap, SLOTS
        else:
            source, target, n = parts.at[s, 1 - core], swap.at[s], s
        return pltpu.make_async_remote_copy(
            src_ref=source, dst_ref=target, send_sem=swap_send.at[n], recv_sem=swap_recv.at[n],
            device_id={"col": partner}, device_id_type=MESH)

    def line_copy(s):
        if s is None:
            source, rows, n, goal = o_sum, pl.ds(0, 2 * q), SLOTS, r
        else:
            goal, spot = kept(s)
            source, rows, n = summed.at[s], pl.ds(spot, q), s
        return pltpu.make_async_remote_copy(
            src_ref=source, dst_ref=landed.at[z, rows], send_sem=line_send.at[n], recv_sem=line_recv.at[z],
            device_id={"col": 2 * goal + core}, device_id_type=MESH), goal, rows

    def swap_finish(s):
        swap_copy(s).wait_recv()
        if s is None:
            total = o_parts[core] + o_swap[...]
        else:
            total = parts[s, core] + swap[s]
        copy, goal, rows = line_copy(s)

        @pl.when(goal == z)
        def _():
            landed[z, rows] = total

        @pl.when(goal != z)
        def _():
            if s is None:
                o_sum[...] = total
            else:
                summed[s] = total
            copy.start()

    def store(s, value):
        parts[s, 0] = value[:q]
        parts[s, 1] = value[q:]
        swap_copy(s).start()

    t_copy.wait()
    total = None
    for i, (at, width) in enumerate(cuts):
        v_copies[i].wait()
        term = lax.dot_general(
            t[:pairs, at:at + width], v[:, at:at + width], NT, preferred_element_type=jnp.float32)
        total = term if total is None else total + term
    o_parts[0] = total[:2 * q]
    o_parts[1] = total[2 * q:]
    swap_copy(None).start()
    heard(0, 1)
    signal_line(known.at[2], known.at[3])
    heard(2, 3)
    swap_finish(None)

    for s in range(SLOTS - 1):
        if s < 3:
            arrive(s, None)
        else:
            for n in range(len(cuts)):
                arrive(s, n)
        if s < 2:
            for link in range(2):
                start(link, (R1, R2)[s])
        if s == 1:
            for link in range(2):
                @pl.when(own_last[link])
                def _():
                    start(link, L2)
        store(s, multiply(s, 0, t_ref.shape[1]))
        if s > 0:
            swap_finish(s - 1)

    s = SLOTS - 1
    total = None
    for n, (at, width) in enumerate(cuts):
        arrive(s, n)
        term = multiply(s, at, width)
        total = term if total is None else total + term
        if n == 0:
            swap_finish(s - 1)
    store(s, total)
    swap_finish(s)

    for source in range(chips):
        @pl.when(z != source)
        def _():
            pltpu.make_async_copy(landed.at[source], landed.at[source], line_recv.at[source]).wait()
    total = landed[0]
    for source in range(1, chips):
        total = total + landed[source]
    out_ref[...] = total.astype(out_ref.dtype)

    for link in range(2):
        for item in range(6):
            for copy in items[link][item]:
                copy.wait_send()
    for s in [None, *range(SLOTS)]:
        swap_copy(s).wait_send()
        copy, goal, _ = line_copy(s)

        @pl.when(goal != z)
        def _():
            copy.wait_send()


def ladder_on_chips(integrals, amplitudes):
    chips = lax.axis_size("col") // 2
    blocks = amplitudes.T
    pairs, depth = blocks.shape
    rows = integrals.shape[0]
    q = pairs // 4
    cuts = cuts_of(depth, 4, 256)
    f32 = jnp.float32
    dma = pltpu.SemaphoreType.DMA
    return pl.pallas_call(
        functools.partial(ladder_kernel, chips, cuts),
        out_shape=jax.ShapeDtypeStruct((2 * q, rows), jnp.bfloat16),
        in_specs=[pl.BlockSpec(memory_space=pl.ANY)] * 2,
        out_specs=pl.BlockSpec(memory_space=pltpu.VMEM),
        scratch_shapes=[
            pltpu.VMEM((rows, depth), jnp.bfloat16),
            pltpu.VMEM((4 * pairs, depth), jnp.bfloat16),
            pltpu.VMEM((2, 2 * q, rows), f32),
            pltpu.VMEM((2 * q, rows), f32),
            pltpu.VMEM((2 * q, rows), f32),
            pltpu.VMEM((SLOTS, 2, q, rows), f32),
            pltpu.VMEM((SLOTS, q, rows), f32),
            pltpu.VMEM((SLOTS, q, rows), f32),
            pltpu.VMEM((chips, 2 * q, rows), f32),
            dma((len(cuts),)), dma,
            dma((2, 6, len(cuts))), dma((2, 6, len(cuts))),
            dma((SLOTS + 1,)), dma((SLOTS + 1,)),
            dma((SLOTS + 1,)), dma((chips,)),
            pltpu.SemaphoreType.REGULAR((4,)),
        ],
        compiler_params=pltpu.CompilerParams(
            collective_id=0, has_side_effects=True, vmem_limit_bytes=67043328),
    )(integrals, blocks)


def per_device(integrals, amplitudes):
    columns = lax.axis_size("col")
    if lax.axis_size("row") == 4 and columns == 8 and amplitudes.shape[1] % 64 == 0:
        return ladder_on_chips(integrals, amplitudes)
    gathered = lax.all_gather(amplitudes, "row", axis=1, tiled=True)
    product = lax.dot_general(
        gathered, integrals, (((0,), (1,)), ((), ())), preferred_element_type=jnp.float32)
    return lax.psum_scatter(product, "col", scatter_dimension=0, tiled=True).astype(jnp.bfloat16)


def solution(mesh):
    in_specs = (P("row", "col"), P("col", "row"))
    out_specs = P("col", "row")
    return jax.shard_map(
        per_device, mesh=mesh, in_specs=in_specs, out_specs=out_specs, check_vma=False
    )
```

time: 28.3 us -> 28.7 us (1.014)
  Pallas kernels: 26.7 us -> 27.1 us
    pallas_call x1, Pallas kernels: 26.7 us -> 27.1 us  [ladder_on_chips(): pl.pallas_call(functools.partial(ladder_kernel, chips, cuts), out_shape=j...]
where the time goes in v1:
time: 28.7 us; the launch traced here: 28.5 us
  Pallas kernels  27.1 us (94%)
  local copies, waits for them, and re-layouts  1.42 us (5%)
    pallas_call x1, Pallas kernels, ladder_on_chips(): pl.pallas_call(functools.partial(ladder_kernel, chips, cuts), out_shape=j...  27.1 us
    unnamed x1, local copies, waits for them, and re-layouts  1.42 us

profile of v1, /device:TPU:4, one launch (start us, length us, event | category | flops | bytes accessed | tf_op | source)
XLA Modules:
  0.0 28.5 jit_solution(1517675574348920190)
XLA Ops:
  0.0 27.1 %shard_map.28 = bf16[32,720]{1,0:T(8,128)(2,1)} custom-call(bf16[720,2880]{1,0:T(8,128)(2,1)} %v_ref.1, bf16[64,2880]{1,0:T(8,128)(2,1)} %bitcast.1), custom_call_target="tpu_custom_call" | custom-call | tf_op jit(solution)/shard_map/pallas_call | solution.py:279
  27.1 1.4 %copy.4 = bf16[32,720]{1,0:T(8,128)(2,1)} copy(bf16[32,720]{1,0:T(8,128)(2,1)} %shard_map.28) | data formatting | bytes 92160

commit v2 on v0

--- a/solution.py
+++ b/solution.py
@@ -18,7 +18,7 @@
 
 def ladder_kernel(chips, cuts, v_ref, t_ref, out_ref, v, t, parts, swap, summed, landed,
                   v_sem, t_sem, near_send, near_recv, far_send, far_recv, late_send, late_recv, last_send, last_recv,
-                  swap_send, swap_recv, line_send, line_recv):
+                  swap_send, swap_recv, line_send, line_recv, known):
     depth = t_ref.shape[1]
     half = t_ref.shape[0] // 2
     part = half // 2
@@ -46,10 +46,29 @@
     pl.semaphore_signal(barrier, inc=1, device_id={"row": rx}, device_id_type=MESH)
     pl.semaphore_signal(barrier, inc=1, device_id={"row": ry}, device_id_type=MESH)
     pl.semaphore_signal(barrier, inc=1, device_id={"col": 2 * z + other}, device_id_type=MESH)
-    for step in range(1, chips):
-        peer = lax.rem(z + step, chips)
-        pl.semaphore_signal(barrier, inc=1, device_id={"col": 2 * peer + core}, device_id_type=MESH)
-    pl.semaphore_wait(barrier, chips + 2)
+    above, below = z < chips - 1, z > 0
+
+    def signal_line(up, down):
+        @pl.when(above)
+        def _():
+            pl.semaphore_signal(up, inc=1, device_id={"col": c + 2}, device_id_type=MESH)
+
+        @pl.when(below)
+        def _():
+            pl.semaphore_signal(down, inc=1, device_id={"col": c - 2}, device_id_type=MESH)
+
+    def heard(first, second):
+        @pl.when(below)
+        def _():
+            pl.semaphore_wait(known.at[first], 1)
+
+        @pl.when(above)
+        def _():
+            pl.semaphore_wait(known.at[second], 1)
+
+    signal_line(barrier, barrier)
+    pl.semaphore_wait(barrier, 5 - jnp.where(above, 0, 1) - jnp.where(below, 0, 1))
+    signal_line(known.at[0], known.at[1])
 
     def send(source, target, to, sems):
         copy = pltpu.make_async_remote_copy(
@@ -131,6 +150,9 @@
         total = term if total is None else total + term
     store(0, total)
     swaps = [swap_start(0)]
+    heard(0, 1)
+    signal_line(known.at[2], known.at[3])
+    heard(2, 3)
 
     wait(near_copies[:2])
     far_copies = relay(0)
@@ -219,6 +241,7 @@
             dma((len(cuts), 2)), dma((len(cuts), 2)),
             dma((5,)), dma((5,)),
             dma((5,)), dma((chips,)),
+            pltpu.SemaphoreType.REGULAR((4,)),
         ],
         compiler_params=pltpu.CompilerParams(
             collective_id=0, has_side_effects=True, vmem_limit_bytes=67043328),

time: 28.3 us -> 27.2 us (0.961)
  Pallas kernels: 26.7 us -> 25.6 us
    pallas_call x1, Pallas kernels: 26.7 us -> 25.6 us  [ladder_on_chips(): pl.pallas_call(functools.partial(ladder_kernel, chips, cuts), out_shape=j...]
where the time goes in v2:
time: 27.2 us; the launch traced here: 27 us
  Pallas kernels  25.6 us (94%)
  local copies, waits for them, and re-layouts  1.42 us (5%)
    pallas_call x1, Pallas kernels, ladder_on_chips(): pl.pallas_call(functools.partial(ladder_kernel, chips, cuts), out_shape=j...  25.6 us
    unnamed x1, local copies, waits for them, and re-layouts  1.42 us

profile of v2, /device:TPU:4, one launch (start us, length us, event | category | flops | bytes accessed | tf_op | source)
XLA Modules:
  0.0 27.0 jit_solution(9011396238323117053)
XLA Ops:
  0.0 25.6 %shard_map.28 = bf16[32,720]{1,0:T(8,128)(2,1)} custom-call(bf16[720,2880]{1,0:T(8,128)(2,1)} %v_ref.1, bf16[64,2880]{1,0:T(8,128)(2,1)} %bitcast.1), custom_call_target="tpu_custom_call" | custom-call | tf_op jit(solution)/shard_map/pallas_call | solution.py:225
  25.6 1.4 %copy.4 = bf16[32,720]{1,0:T(8,128)(2,1)} copy(bf16[32,720]{1,0:T(8,128)(2,1)} %shard_map.28) | data formatting | bytes 92160
